TPU v7x, 512 devices: a whole 4x4x16 slice. The times are simulated.
512 devices in a mesh: dp: 32 (over z, core), vocab: 16 (over y, x).
Axes of the slice: x: 4, y: 4, z: 16, core: 2. Of those that a mesh axis runs over, the one named last changes fastest.
Arguments:
- student_hidden: bfloat16 [192, 5120], P('dp', 'vocab'), may hold values from -71 to 71
- teacher_hidden: bfloat16 [192, 4096], P('dp', 'vocab'), may hold values from -73 to 73
- student_head: bfloat16 [90112, 5120], P(('dp', 'vocab')), may hold values from -16 to 16
- teacher_head: bfloat16 [90112, 4096], P(('dp', 'vocab')), may hold values from -16 to 16
Outputs:
- hidden_grad: bfloat16 [192, 5120], P('dp', 'vocab')
- head_grad: bfloat16 [90112, 5120], P(('dp', 'vocab'))
All inputs are finite; a program needn't handle non-finite values.
Results may differ from a plain program's by a relative error of at most 0.017.
Values may be sent and summed in bfloat16 or wider, within the bound.
A program may use at most 64 MiB of HBM per device.

v0:
```python
import jax
import jax.numpy as jnp
from jax import lax
from jax.sharding import PartitionSpec as P


def on_device(student_hidden, teacher_hidden, student_head, teacher_head):
    student_part, teacher_part = (
        lax.all_gather(student_hidden, "vocab", axis=1, tiled=True),
        lax.all_gather(teacher_hidden, "vocab", axis=1, tiled=True),
    )
    hidden_full = lax.all_gather(student_part, "dp", axis=0, tiled=True)
    student_logits = lax.dot_general(
        hidden_full, student_head, (((1,), (1,)), ((), ())), preferred_element_type=jnp.float32
    )
    teacher_logits = lax.dot_general(
        lax.all_gather(teacher_part, "dp", axis=0, tiled=True),
        teacher_head,
        (((1,), (1,)), ((), ())),
        preferred_element_type=jnp.float32,
    )
    student_peak, teacher_peak = lax.pmax(
        (
            jnp.max(student_logits, axis=1, keepdims=True),
            jnp.max(teacher_logits, axis=1, keepdims=True),
        ),
        ("dp", "vocab"),
    )
    student_total, teacher_total = lax.psum(
        (
            jnp.sum(jnp.exp(student_logits - student_peak), axis=1, keepdims=True),
            jnp.sum(jnp.exp(teacher_logits - teacher_peak), axis=1, keepdims=True),
        ),
        ("dp", "vocab"),
    )
    log_student = student_logits - (student_peak + jnp.log(student_total))
    log_teacher = teacher_logits - (teacher_peak + jnp.log(teacher_total))
    probs = jnp.exp(log_student)
    gap = log_student - log_teacher
    divergence = lax.psum(jnp.sum(probs * gap, axis=1, keepdims=True), ("dp", "vocab"))
    logit_grad = (probs * (gap - divergence)).astype(jnp.bfloat16)
    partial_rows = lax.psum_scatter(
        jnp.dot(logit_grad, student_head, preferred_element_type=jnp.float32).astype(jnp.bfloat16),
        "dp",
        scatter_dimension=0,
        tiled=True,
    )
    hidden_grad = lax.psum_scatter(partial_rows, "vocab", scatter_dimension=1, tiled=True)
    head_grad = lax.dot_general(
        logit_grad, hidden_full, (((0,), (0,)), ((), ())), preferred_element_type=jnp.float32
    ).astype(jnp.bfloat16)
    return (hidden_grad, head_grad)


def solution(mesh):
    return jax.shard_map(
        on_device,
        mesh=mesh,
        in_specs=(
            P("dp", "vocab"),
            P("dp", "vocab"),
            P(("dp", "vocab"), None),
            P(("dp", "vocab"), None),
        ),
        out_specs=(P("dp", "vocab"), P(("dp", "vocab"), None)),
        check_vma=False,
    )
```

profile of v0, /device:TPU:2, one launch (start us, length us, event | category | flops | bytes accessed | tf_op | source)
XLA Modules:
  0.0 681.1 jit_solution(2673088508616346670)
XLA Ops:
  7.2 28.4 %all_gather.14 = bf16[6,4096]{1,0:T(8,128)(2,1)} all-gather(bf16[6,256]{1,0:T(8,128)(2,1)} %param.5), channel_id=1, replica_groups=mesh['dp'=32,'vocab'=16] {'vocab'}, dimensions={1}, use_global_device_ids=true | all-gather | bytes 52224 | tf_op jit(solution)/shard_map/all_gather | solution.py:10
  35.7 21.7 %all-gather = bf16[16,320,6]{1,2,0:T(8,128)(2,1)S(1)} all-gather(bf16[1,320,6]{1,2,0:T(8,128)(2,1)} %bitcast.38), channel_id=1, replica_groups=mesh['dp'=32,'vocab'=16] {'vocab'}, dimensions={0}, use_global_device_ids=true | all-gather | bytes 65280 | tf_op jit(solution)/shard_map/all_gather | solution.py:9
  57.4 0.8 reshape.6
  58.3 48.6 %all-gather.8.cloned.1.call-done = bf16[32,6,4096]{2,1,0:T(8,128)(2,1)} async-done(((bf16[1,6,4096]{2,1,0:T(8,128)(2,1)}), bf16[32,6,4096]{2,1,0:T(8,128)(2,1)}) %all-gather.8.cloned.1.call-update) | async-done | bytes 1572880 | tf_op jit(solution)/shard_map/all_gather | solution.py:17
  106.9 2.5 reshape.10
  109.5 2.5 fusion.1
  112.0 66.8 %all-gather.6.cloned.1.call-done = bf16[32,6,5120]{2,1,0:T(8,128)(2,1)} async-done(((bf16[1,6,5120]{2,1,0:T(8,128)(2,1)}), bf16[32,6,5120]{2,1,0:T(8,128)(2,1)}) %all-gather.6.cloned.1.call-update) | async-done | bytes 1966096 | tf_op jit(solution)/shard_map/all_gather | solution.py:12
  178.8 4.1 reshape.8
  182.9 2.3 fusion.2
  185.2 101.6 %all-reduce.3 = (f32[192,1]{0,1:T(1,128)S(1)}, f32[192,1]{0,1:T(1,128)S(1)}) all-reduce(f32[192,1]{0,1:T(1,128)S(1)} %bitcast.39, f32[192,1]{0,1:T(1,128)S(1)} %bitcast.40), channel_id=1, replica_groups=mesh['dp'=32,'vocab'=16] {'dp','vocab'}, use_global_device_ids=true, to_apply=%region_5.0 | all-reduce | flops 384 | bytes 3072 | tf_op jit(solution)/shard_map/pmax | solution.py:22
  286.8 0.1 exponential_reduce_fusion.1
  286.9 0.1 exponential_reduce_fusion
  286.9 99.4 %all-reduce.2 = (f32[192,1]{0,1:T(1,128)S(1)}, f32[192,1]{0,1:T(1,128)S(1)}) all-reduce(f32[192,1]{0,1:T(1,128)S(1)} %bitcast.42, f32[192,1]{0,1:T(1,128)S(1)} %bitcast.41), channel_id=1, replica_groups=mesh['dp'=32,'vocab'=16] {'dp','vocab'}, use_global_device_ids=true, to_apply=%region_7.0 | all-reduce | flops 384 | bytes 3072 | tf_op jit(solution)/shard_map/psum | solution.py:29
  386.3 0.1 multiply_reduce_fusion
  386.4 100.2 %psum.23 = f32[192]{0:T(256)S(1)} all-reduce(f32[192]{0:T(256)S(1)} %multiply_reduce_fusion), channel_id=1, replica_groups=mesh['dp'=32,'vocab'=16] {'dp','vocab'}, use_global_device_ids=true, to_apply=%region_9.0 | all-reduce | flops 192 | bytes 1536 | tf_op jit(solution)/shard_map/psum | solution.py:40
  486.6 0.1 multiply_convert_fusion
  486.7 2.0 convolution_convert_fusion
  488.7 59.0 %fusion = bf16[8,5120]{1,0:T(8,128)(2,1)S(1)} fusion(bf16[192,5120]{1,0:T(8,128)(2,1)} %convolution_convert_fusion), kind=kCustom, calls=%all-reduce-scatter | all-reduce-scatter fusion | flops 1310721 | bytes 2050048
  547.7 1.3 collective-permute-start.6
  549.0 2.1 collective-permute-start.5
  551.2 5.4 collective-permute-start.7
  556.6 4.7 collective-permute-start.4
  561.3 4.8 collective-permute-start.3
  566.1 1.8 collective-permute-start.2
  567.9 2.9 collective-permute-start.1
  570.8 4.1 collective-permute-start
  574.9 1.3 dynamic-slice.4
  576.8 2.3 concatenate
  579.2 1.6 copy.8
  580.8 3.4 convolution_convert_fusion.1
  584.2 88.8 %reduce-scatter.6.cloned.1.call-done = bf16[320,6]{1,0:T(8,128)(2,1)} async-done(((bf16[5120,6]{1,0:T(8,128)(2,1)}), bf16[320,6]{1,0:T(8,128)(2,1)}) %reduce-scatter.6.cloned.1.call-update) | async-done | bytes 3856
  673.0 1.6 copy.9
  (22 shorter events, 0.3 us)
Async XLA Ops:
  7.2 175.8 %copy-start = (bf16[176,5120]{1,0:T(8,128)(2,1)S(1)}, bf16[176,5120]{1,0:T(8,128)(2,1)}, u32[]{:S(2)}) copy-start(bf16[176,5120]{1,0:T(8,128)(2,1)} %param.6) | copy-start | bytes 5406724
  7.2 99.7 %all-gather.8.cloned.1.call-start = ((), (), s32[]{:S(2)}) async-start(), calls=%async_computation.2 | async-start | bytes 2162688 | tf_op jit(solution)/shard_map/all_gather | solution.py:17
  35.6 143.1 %all-gather.6.cloned.1.call-start = ((), (), s32[]{:S(2)}) async-start(), calls=%async_computation.1 | async-start | bytes 2703360 | tf_op jit(solution)/shard_map/all_gather | solution.py:12
  58.2 614.8 %reduce-scatter.6.cloned.1.call-start = ((), (), s32[]{:S(2)}) async-start(), calls=%async_computation.3 | async-start | bytes 1392640
  182.9 2.3 copy-start.1
  547.7 20.2 %collective-permute-start.6 = (bf16[8,5120]{1,0:T(8,128)(2,1)S(1)}, bf16[8,5120]{1,0:T(8,128)(2,1)S(1)}, u32[]{:S(2)}, u32[]{:S(2)}) collective-permute-start(bf16[8,5120]{1,0:T(8,128)(2,1)S(1)} %fusion), channel_id=1, source_target_pairs={{0,112},{16,128},{32,144},{48,160},{64,176},{80,192},{96,208},{112... | collective-permute-start | bytes 245768
  549.0 21.8 %collective-permute-start.5 = (bf16[8,5120]{1,0:T(8,128)(2,1)S(1)}, bf16[8,5120]{1,0:T(8,128)(2,1)S(1)}, u32[]{:S(2)}, u32[]{:S(2)}) collective-permute-start(bf16[8,5120]{1,0:T(8,128)(2,1)S(1)} %fusion), channel_id=1, source_target_pairs={{0,96},{16,112},{32,128},{48,144},{64,160},{80,176},{96,192},{112,... | collective-permute-start | bytes 245768
  551.2 14.9 %collective-permute-start.7 = (bf16[6,5120]{1,0:T(8,128)(2,1)S(1)}, bf16[6,5120]{1,0:T(8,128)(2,1)S(1)}, u32[]{:S(2)}, u32[]{:S(2)}) collective-permute-start(bf16[6,5120]{1,0:T(8,128)(2,1)S(1)} %slice), channel_id=1, source_target_pairs={{0,128},{16,144},{32,160},{48,176},{64,192},{80,208},{96,224},{112... | collective-permute-start | bytes 184328
  556.6 20.2 %collective-permute-start.4 = (bf16[8,5120]{1,0:T(8,128)(2,1)S(1)}, bf16[8,5120]{1,0:T(8,128)(2,1)S(1)}, u32[]{:S(2)}, u32[]{:S(2)}) collective-permute-start(bf16[8,5120]{1,0:T(8,128)(2,1)S(1)} %fusion), channel_id=1, source_target_pairs={{0,80},{16,96},{32,112},{48,128},{64,144},{80,160},{96,176},{112,1... | collective-permute-start | bytes 245768
  561.3 15.5 %collective-permute-start.3 = (bf16[8,5120]{1,0:T(8,128)(2,1)S(1)}, bf16[8,5120]{1,0:T(8,128)(2,1)S(1)}, u32[]{:S(2)}, u32[]{:S(2)}) collective-permute-start(bf16[8,5120]{1,0:T(8,128)(2,1)S(1)} %fusion), channel_id=1, source_target_pairs={{0,64},{16,80},{32,96},{48,112},{64,128},{80,144},{96,160},{112,17... | collective-permute-start | bytes 245768
  566.1 10.7 %collective-permute-start.2 = (bf16[8,5120]{1,0:T(8,128)(2,1)S(1)}, bf16[8,5120]{1,0:T(8,128)(2,1)S(1)}, u32[]{:S(2)}, u32[]{:S(2)}) collective-permute-start(bf16[8,5120]{1,0:T(8,128)(2,1)S(1)} %fusion), channel_id=1, source_target_pairs={{0,48},{16,64},{32,80},{48,96},{64,112},{80,128},{96,144},{112,160... | collective-permute-start | bytes 245768
  567.9 8.9 %collective-permute-start.1 = (bf16[8,5120]{1,0:T(8,128)(2,1)S(1)}, bf16[8,5120]{1,0:T(8,128)(2,1)S(1)}, u32[]{:S(2)}, u32[]{:S(2)}) collective-permute-start(bf16[8,5120]{1,0:T(8,128)(2,1)S(1)} %fusion), channel_id=1, source_target_pairs={{0,32},{16,48},{32,64},{48,80},{64,96},{80,112},{96,128},{112,144}... | collective-permute-start | bytes 245768
  570.8 6.0 collective-permute-start
Sparse Core Ops, SparseCore 0:
  35.8 71.0 all-gather.7
  109.6 69.1 all-gather.5
  580.9 91.9 reduce-scatter.5
where the time goes:
time: 682 us; the launch traced here: 681 us
  blocking collectives  410 us (60%)
  waiting for transfers between devices  204 us (30%)
  starting transfers between devices  27.2 us (4%)
  between operations  14.6 us (2%)
  local copies, waits for them, and re-layouts  14.3 us (2%)
  matrix products  10.2 us (1%)
    pmax x1, blocking collectives, on_device(): lax.pmax((jnp.max(student_logits, axis=1, keepdims=True), jnp.max(teacher...  102 us
    psum x1, blocking collectives, on_device(): lax.psum(jnp.sum(probs * gap, axis=1, keepdims=True), ('dp', 'vocab'))  100 us
    psum x1, blocking collectives, on_device(): lax.psum((jnp.sum(jnp.exp(student_logits - student_peak), axis=1, keepdim...  99.4 us
    unnamed x12, waiting for transfers between devices  88.8 us
    all_gather x1, waiting for transfers between devices, on_device(): hidden_full = lax.all_gather(student_part, 'dp', axis=0, tiled=True)  66.8 us
    unnamed x1, blocking collectives  59 us
    all_gather x1, waiting for transfers between devices, on_device(): lax.all_gather(teacher_part, 'dp', axis=0, tiled=True)  48.6 us
    all_gather x1, blocking collectives, on_device(): lax.all_gather(teacher_hidden, 'vocab', axis=1, tiled=True)  28.4 us
  transfers between devices with their start and end apart: 11, of which 3 were waited for; matrix products, arithmetic and copies ran while one was open for 2% of the time, Pallas kernels for 0%

commit v1 on v0

v1 whole, which is shorter than its diff:
```python
import functools

import jax
import jax.numpy as jnp
from jax import lax
from jax.experimental import pallas as pl
from jax.experimental.pallas import tpu as pltpu
from jax.sharding import PartitionSpec as P

MESH = pl.DeviceIdType.MESH
F32 = jnp.float32
BF16 = jnp.bfloat16
R = 6
FS, FT = 320, 256
WS = 384
W = WS + FT
TP = 128
NEG = ((1,), (1,))


def merge_stats(parts):
    m, s, a, mt, st = (parts[:, i : i + 1, :] for i in range(5))
    top = jnp.max(m, axis=0, keepdims=True)
    top_t = jnp.max(mt, axis=0, keepdims=True)
    w = jnp.exp(m - top)
    total = jnp.sum(w * s, axis=0)
    total_t = jnp.sum(jnp.exp(mt - top_t) * st, axis=0)
    weighted = jnp.sum(w * (a + s * ((m - top) - (mt - top_t))), axis=0)
    zero = jnp.zeros_like(total)
    return jnp.concatenate([top[0], total, weighted, top_t[0], total_t, zero, zero, zero], axis=0)


def kernel(
    Z, Y, X,
    own_ref, sw_hbm, tw_hbm,
    hg_ref, hd_hbm,
    zb, zf, hb, sw, tw, ls, lt, g, sc, sx, sy, sz,
    pown, psend, precv, ps, ra, rb, qa, qb, ra2, rb2, fz, zs, zr, ob,
    wsem, z_s, z_r, a1_s, a1_r, b1_s, b1_r, a2_s, a2_r, b2_s, b2_r, d_s, d_r,
    tc_s, tc_r, tx_s, tx_r, ty_s, ty_r, tz_s, tz_r,
    pc_s, pc_r, ra_s, ra_r, rb_s, rb_r, ra2_s, ra2_r, rb2_s, rb2_r, rz_s, rz_r, osem,
):
    dp, vocab = lax.axis_index("dp"), lax.axis_index("vocab")
    z, c = dp // 2, dp % 2
    y, x = vocab // X, vocab % X
    n = Z * R
    h = n // 2
    QL = X * FS
    NP = Y * X // 2

    def at_z(k):
        return (lax.rem(z + k, Z) * 2 + c, vocab)

    def at_x(k):
        return (dp, y * X + lax.rem(x + k, X))

    def at_y(k):
        return (dp, lax.rem(y + k, Y) * X + x)

    partner = (z * 2 + 1 - c, vocab)

    def copy(src, dst, s, r, dev):
        return pltpu.make_async_remote_copy(
            src_ref=src, dst_ref=dst, send_sem=s, recv_sem=r, device_id=dev, device_id_type=MESH
        )

    w_copy = pltpu.make_async_copy(sw_hbm, sw, wsem.at[0])
    t_copy = pltpu.make_async_copy(tw_hbm, tw, wsem.at[1])
    w_copy.start()
    t_copy.start()

    barrier = pltpu.get_barrier_semaphore()
    for k in range(1, Z):
        pl.semaphore_signal(barrier, inc=1, device_id=at_z(k), device_id_type=MESH)
    for k in range(1, X):
        pl.semaphore_signal(barrier, inc=1, device_id=at_x(k), device_id_type=MESH)
    for k in range(1, Y):
        pl.semaphore_signal(barrier, inc=1, device_id=at_y(k), device_id_type=MESH)
    pl.semaphore_signal(barrier, inc=1, device_id=partner, device_id_type=MESH)
    zb[z] = own_ref[...]
    pl.semaphore_wait(barrier, Z + X + Y - 2)

    zorder = sorted(range(1, Z), key=lambda k: -min(k, Z - k))
    for k in zorder:
        copy(zb.at[z], zb.at[z], z_s.at[k], z_r.at[k], at_z(k)).start()
    for k in reversed(zorder):
        slot = lax.rem(z + Z - k, Z)
        copy(zb.at[slot], zb.at[slot], z_s.at[k], z_r.at[k], at_z(k)).wait_recv()
    for i in range(Z):
        zf[R * i : R * i + R, :] = zb[i, 0:R, :].astype(F32)
    hb[c, y, x] = zf[...].astype(BF16)

    def blk(cc, yy, xx, half):
        return hb.at[cc, yy, xx, pl.ds(half * h, h), :]

    def a1(xx, k):
        return copy(blk(c, y, xx, 0), blk(c, y, xx, 0), a1_s.at[k], a1_r.at[k], at_x(k))

    def b1(yy, k):
        return copy(blk(c, yy, x, 1), blk(c, yy, x, 1), b1_s.at[k], b1_r.at[k], at_y(k))

    def a2(yy, xx, k, i):
        return copy(blk(c, yy, xx, 0), blk(c, yy, xx, 0), a2_s.at[k, i], a2_r.at[k, i], at_y(k))

    def b2(yy, xx, k, i):
        return copy(blk(c, yy, xx, 1), blk(c, yy, xx, 1), b2_s.at[k, i], b2_r.at[k, i], at_x(k))

    def fwd(cc, yy, xx, half):
        return copy(blk(cc, yy, xx, half), blk(cc, yy, xx, half), d_s.at[half, yy, xx], d_r.at[half, yy, xx], partner)

    near_x = sorted(range(1, X), key=lambda k: min(k, X - k))
    near_y = sorted(range(1, Y), key=lambda k: min(k, Y - k))
    for k in reversed(near_x):
        a1(x, k).start()
    for k in reversed(near_y):
        b1(y, k).start()
    for k in reversed(near_y):
        a2(y, x, k, 0).start()
    for k in reversed(near_x):
        b2(y, x, k, 0).start()
    fwd(c, y, x, 0).start()
    fwd(c, y, x, 1).start()
    for k in range(max(X, Y) - 1):
        if k < X - 1:
            i = near_x[k]
            xx = lax.rem(x + X - i, X)
            a1(xx, i).wait_recv()
            for kk in reversed(near_y):
                a2(y, xx, kk, i).start()
            fwd(c, y, xx, 0).start()
        if k < Y - 1:
            i = near_y[k]
            yy = lax.rem(y + Y - i, Y)
            b1(yy, i).wait_recv()
            for kk in reversed(near_x):
                b2(yy, x, kk, i).start()
            fwd(c, yy, x, 1).start()
    order_x = [0] + near_x
    order_y = [0] + near_y
    for i in order_x:
        for k in near_y:
            yy, xx = lax.rem(y + Y - k, Y), lax.rem(x + X - i, X)
            a2(yy, xx, k, i).wait_recv()
            fwd(c, yy, xx, 0).start()
    for i in order_y:
        for k in near_x:
            yy, xx = lax.rem(y + Y - i, Y), lax.rem(x + X - k, X)
            b2(yy, xx, k, i).wait_recv()
            fwd(c, yy, xx, 1).start()

    def each_block(fn):
        @pl.loop(0, Y)
        def _(yy):
            @pl.loop(0, X)
            def _(xx):
                fn(yy, xx, 0)
                fn(yy, xx, 1)

    each_block(lambda yy, xx, half: fwd(1 - c, yy, xx, half).wait_recv())
    w_copy.wait()
    t_copy.wait()

    fill = TP - n
    pairs_y = X // 2

    def pair(p):
        yy, xx = p // pairs_y, (p % pairs_y) * 2
        s, t = [], []
        for cc in range(2):
            even, odd = hb[cc, yy, xx], hb[cc, yy, xx + 1]
            s.append(
                jnp.concatenate([even[:, :256], even[:, 256:384] + odd[:, :128], odd[:, 128:384]], axis=1)
            )
            t.append(jnp.concatenate([even[:, 384:], odd[:, 384:]], axis=1))
            s.append(jnp.zeros((fill, 2 * FS), BF16))
            t.append(jnp.zeros((fill, 2 * FT), BF16))
        return jnp.concatenate(s, axis=0), jnp.concatenate(t, axis=0)

    ls[...] = jnp.zeros_like(ls)
    lt[...] = jnp.zeros_like(lt)

    @pl.loop(0, NP)
    def _(p):
        s, t = pair(p)
        at_s = pl.ds(pl.multiple_of(p * (2 * FS), 128), 2 * FS)
        at_t = pl.ds(pl.multiple_of(p * (2 * FT), 128), 2 * FT)
        ls[...] += lax.dot_general(sw[:, at_s], s, (NEG, ((), ())), preferred_element_type=F32)
        lt[...] += lax.dot_general(tw[:, at_t], t, (NEG, ((), ())), preferred_element_type=F32)

    m = jnp.max(ls[...], axis=0, keepdims=True)
    mt = jnp.max(lt[...], axis=0, keepdims=True)
    ds, dt = ls[...] - m, lt[...] - mt
    e = jnp.exp(ds)
    zero = jnp.zeros_like(m)
    sc[c] = jnp.concatenate(
        [
            m,
            jnp.sum(e, axis=0, keepdims=True),
            jnp.sum(e * (ds - dt), axis=0, keepdims=True),
            mt,
            jnp.sum(jnp.exp(dt), axis=0, keepdims=True),
            zero, zero, zero,
        ],
        axis=0,
    )
    copy(sc.at[c], sc.at[c], tc_s, tc_r, partner).start()
    copy(sc.at[1 - c], sc.at[1 - c], tc_s, tc_r, partner).wait_recv()
    sx[x] = merge_stats(sc[...])
    for k in reversed(near_x):
        copy(sx.at[x], sx.at[x], tx_s.at[k], tx_r.at[k], at_x(k)).start()
    for k in near_x:
        slot = lax.rem(x + X - k, X)
        copy(sx.at[slot], sx.at[slot], tx_s.at[k], tx_r.at[k], at_x(k)).wait_recv()
    sy[y] = merge_stats(sx[...])
    for k in reversed(near_y):
        copy(sy.at[y], sy.at[y], ty_s.at[k], ty_r.at[k], at_y(k)).start()
    for k in near_y:
        slot = lax.rem(y + Y - k, Y)
        copy(sy.at[slot], sy.at[slot], ty_s.at[k], ty_r.at[k], at_y(k)).wait_recv()
    sz[z] = merge_stats(sy[...])
    for k in zorder:
        copy(sz.at[z], sz.at[z], tz_s.at[k], tz_r.at[k], at_z(k)).start()
    for k in reversed(zorder):
        slot = lax.rem(z + Z - k, Z)
        copy(sz.at[slot], sz.at[slot], tz_s.at[k], tz_r.at[k], at_z(k)).wait_recv()
    st = merge_stats(sz[...])

    top, total, weighted, top_t, total_t = (st[i : i + 1] for i in range(5))
    log_total, log_total_t = jnp.log(total), jnp.log(total_t)
    divergence = weighted / total - log_total + log_total_t
    log_student = (ls[...] - top) - log_total
    log_teacher = (lt[...] - top_t) - log_total_t
    grad = jnp.exp(log_student) * ((log_student - log_teacher) - divergence)
    lane = lax.broadcasted_iota(jnp.int32, grad.shape, 1)
    grad = jnp.where(lane % TP < n, grad, 0.0).astype(BF16)
    g[...] = grad

    @pl.loop(0, Y)
    def _(i):
        yy = lax.rem(y + 1 + i, Y)

        @pl.loop(0, pairs_y)
        def _(q):
            at_s = pl.ds(pl.multiple_of(yy * QL + q * (2 * FS), 128), 2 * FS)
            rows = lax.dot_general(g[...], sw[:, at_s], (((0,), (0,)), ((), ())), preferred_element_type=F32)
            at_q = pl.ds(pl.multiple_of(q * (2 * FS), 128), 2 * FS)
            lo, hi = rows[0:n], rows[TP : TP + n]
            pown[yy, :, at_q] = jnp.where(c == 0, lo, hi)
            psend[yy, :, at_q] = jnp.where(c == 0, hi, lo).astype(BF16)

        copy(psend.at[yy], precv.at[yy], pc_s.at[yy], pc_r.at[yy], partner).start()

    def win(xx):
        return pl.multiple_of((5 * xx // 2) * 128, 128)

    @pl.loop(0, Y)
    def _(i):
        yy = lax.rem(y + 1 + i, Y)
        copy(psend.at[yy], precv.at[yy], pc_s.at[yy], pc_r.at[yy], partner).wait_recv()
        ps[yy] = (pown[yy] + precv[yy].astype(F32)).astype(BF16)
        for k in reversed(near_x):
            src = ps.at[yy, pl.ds(0, h), pl.ds(win(lax.rem(x + k, X)), WS)]
            copy(src, ra.at[k, yy], ra_s.at[k, yy], ra_r.at[k, yy], at_x(k)).start()

        @pl.when(i < Y - 1)
        def _():
            k = i + 1
            copy(ps.at[yy, pl.ds(h, h), :], rb.at[k], rb_s.at[k], rb_r.at[k], at_y(k)).start()

    @pl.loop(0, NP)
    def _(p):
        s, _t = pair(p)
        at_s = pl.ds(pl.multiple_of(p * (2 * FS), 128), 2 * FS)
        ob[:, at_s] = jnp.dot(g[...], s, preferred_element_type=F32).astype(BF16)
        pltpu.make_async_copy(ob.at[:, at_s], hd_hbm.at[:, at_s], osem.at[p]).start()

    def ra_copy(k, yy):
        return copy(ra.at[k, yy], ra.at[k, yy], ra_s.at[k, yy], ra_r.at[k, yy], at_x(k))

    def rb_copy(k):
        return copy(rb.at[k], rb.at[k], rb_s.at[k], rb_r.at[k], at_y(k))

    for k in near_x:
        @pl.loop(0, Y)
        def _(yy):
            ra_copy(k, yy).wait_recv()

    @pl.loop(0, Y)
    def _(i):
        yy = lax.rem(y + 1 + i, Y)
        acc = ps[yy, 0:h, pl.ds(win(x), WS)].astype(F32)
        for k in range(1, X):
            acc += ra[k, yy].astype(F32)
        qa[yy] = acc.astype(BF16)

        @pl.when(i < Y - 1)
        def _():
            k = i + 1
            copy(qa.at[yy], ra2.at[k], ra2_s.at[k], ra2_r.at[k], at_y(k)).start()

    for k in near_y:
        rb_copy(k).wait_recv()
    acc = ps[y, h : 2 * h, :].astype(F32)
    for k in range(1, Y):
        acc += rb[k].astype(F32)
    qb[...] = acc.astype(BF16)

    def rb2_copy(k):
        src = qb.at[:, pl.ds(win(lax.rem(x + k, X)), WS)]
        return copy(src, rb2.at[k], rb2_s.at[k], rb2_r.at[k], at_x(k))

    def ra2_copy(k):
        return copy(ra2.at[k], ra2.at[k], ra2_s.at[k], ra2_r.at[k], at_y(k))

    for k in reversed(near_x):
        rb2_copy(k).start()
    for k in near_y:
        ra2_copy(k).wait_recv()
    acc = qa[y].astype(F32)
    for k in range(1, Y):
        acc += ra2[k].astype(F32)
    fz[0:h] = acc
    for k in near_x:
        rb2_copy(k).wait_recv()
    acc = qb[:, pl.ds(win(x), WS)].astype(F32)
    for k in range(1, X):
        acc += rb2[k].astype(F32)
    fz[h : 2 * h] = acc

    for i in range(Z):
        zs[i, 0:R, :] = fz[R * i : R * i + R, :].astype(BF16)
        zs[i, R:8, :] = jnp.zeros((8 - R, WS), BF16)
    for k in zorder:
        copy(zs.at[lax.rem(z + k, Z)], zr.at[k], rz_s.at[k], rz_r.at[k], at_z(k)).start()
    for k in reversed(zorder):
        copy(zs.at[lax.rem(z + k, Z)], zr.at[k], rz_s.at[k], rz_r.at[k], at_z(k)).wait_recv()
    acc = zs[z].astype(F32)
    for k in range(1, Z):
        acc += zr[k].astype(F32)
    hg_ref[...] = acc.astype(BF16)

    for k in zorder:
        copy(zb.at[z], zb.at[z], z_s.at[k], z_r.at[k], at_z(k)).wait_send()
        copy(sz.at[z], sz.at[z], tz_s.at[k], tz_r.at[k], at_z(k)).wait_send()
        copy(zs.at[0], zr.at[k], rz_s.at[k], rz_r.at[k], at_z(k)).wait_send()
    for k in near_x:
        a1(x, k).wait_send()
        copy(sx.at[x], sx.at[x], tx_s.at[k], tx_r.at[k], at_x(k)).wait_send()
        rb2_copy(k).wait_send()
        for i in order_y:
            b2(lax.rem(y + Y - i, Y), x, k, i).wait_send()

        @pl.loop(0, Y)
        def _(yy):
            ra_copy(k, yy).wait_send()

    for k in near_y:
        b1(y, k).wait_send()
        copy(sy.at[y], sy.at[y], ty_s.at[k], ty_r.at[k], at_y(k)).wait_send()
        ra2_copy(k).wait_send()
        rb_copy(k).wait_send()
        for i in order_x:
            a2(y, lax.rem(x + X - i, X), k, i).wait_send()
    each_block(lambda yy, xx, half: fwd(c, yy, xx, half).wait_send())
    copy(sc.at[c], sc.at[c], tc_s, tc_r, partner).wait_send()

    @pl.loop(0, Y)
    def _(yy):
        copy(psend.at[yy], precv.at[yy], pc_s.at[yy], pc_r.at[yy], partner).wait_send()

    @pl.loop(0, NP)
    def _(p):
        at_s = pl.ds(pl.multiple_of(p * (2 * FS), 128), 2 * FS)
        pltpu.make_async_copy(ob.at[:, at_s], hd_hbm.at[:, at_s], osem.at[p]).wait()


def build(mesh, Z, Y, X):
    def on_device(sh, th, sw, tw):
        n = Z * R
        h = n // 2
        V, D = sw.shape
        DT = tw.shape[1]
        QL = X * FS
        odd = lax.axis_index("vocab") % 2 == 1
        rows = ((0, 8 - R),)
        stud = jnp.where(
            odd, jnp.pad(sh, rows + ((WS - FS, 0),)), jnp.pad(sh, rows + ((0, WS - FS),))
        )
        own = jnp.concatenate([stud, jnp.pad(th, rows + ((0, 0),))], axis=1)
        V2 = lambda s, d: pltpu.VMEM(s, d)
        DMA = pltpu.SemaphoreType.DMA
        scratch = [
            V2((Z, 8, W), BF16),
            V2((n, W), F32),
            V2((2, Y, X, n, W), BF16),
            V2((V, D), BF16),
            V2((V, DT), BF16),
            V2((V, 2 * TP), F32),
            V2((V, 2 * TP), F32),
            V2((V, 2 * TP), BF16),
            V2((2, 8, 2 * TP), F32),
            V2((X, 8, 2 * TP), F32),
            V2((Y, 8, 2 * TP), F32),
            V2((Z, 8, 2 * TP), F32),
            V2((Y, n, QL), F32),
            V2((Y, n, QL), BF16),
            V2((Y, n, QL), BF16),
            V2((Y, n, QL), BF16),
            V2((X, Y, h, WS), BF16),
            V2((Y, h, QL), BF16),
            V2((Y, h, WS), BF16),
            V2((h, QL), BF16),
            V2((Y, h, WS), BF16),
            V2((X, h, WS), BF16),
            V2((n, WS), F32),
            V2((Z, 8, WS), BF16),
            V2((Z, 8, WS), BF16),
            V2((V, D), BF16),
            DMA((2,)),
            DMA((Z,)), DMA((Z,)),
            DMA((X,)), DMA((X,)), DMA((Y,)), DMA((Y,)),
            DMA((Y, X)), DMA((Y, X)), DMA((X, Y)), DMA((X, Y)),
            DMA((2, Y, X)), DMA((2, Y, X)),
            DMA, DMA, DMA((X,)), DMA((X,)), DMA((Y,)), DMA((Y,)), DMA((Z,)), DMA((Z,)),
            DMA((Y,)), DMA((Y,)),
            DMA((X, Y)), DMA((X, Y)), DMA((Y,)), DMA((Y,)),
            DMA((Y,)), DMA((Y,)), DMA((X,)), DMA((X,)),
            DMA((Z,)), DMA((Z,)), DMA((Y * X // 2,)),
        ]
        hg, hd = pl.pallas_call(
            functools.partial(kernel, Z, Y, X),
            out_shape=(
                jax.ShapeDtypeStruct((8, WS), BF16),
                jax.ShapeDtypeStruct((V, D), BF16),
            ),
            in_specs=[
                pl.BlockSpec(memory_space=pltpu.VMEM),
                pl.BlockSpec(memory_space=pl.ANY),
                pl.BlockSpec(memory_space=pl.ANY),
            ],
            out_specs=(pl.BlockSpec(memory_space=pltpu.VMEM), pl.BlockSpec(memory_space=pl.ANY)),
            scratch_shapes=scratch,
            compiler_params=pltpu.CompilerParams(
                collective_id=0, has_side_effects=True, vmem_limit_bytes=56 << 20
            ),
        )(own, sw, tw)
        hg = jnp.where(odd, hg[:R, WS - FS :], hg[:R, :FS])
        return hg, hd

    return jax.shard_map(
        on_device,
        mesh=mesh,
        in_specs=(
            P("dp", "vocab"),
            P("dp", "vocab"),
            P(("dp", "vocab"), None),
            P(("dp", "vocab"), None),
        ),
        out_specs=(P("dp", "vocab"), P(("dp", "vocab"), None)),
        check_vma=False,
    )


def solution(mesh):
    return build(mesh, mesh.shape["dp"] // 2, 4, mesh.shape["vocab"] // 4)
```

time: 682 us -> 95.1 us (0.14)
  blocking collectives: 410 us -> 0 us
  waiting for transfers between devices: 204 us -> 0 us
  Pallas kernels: 0 us -> 87.6 us
  starting transfers between devices: 27.2 us -> 0 us
  between operations: 14.6 us -> 0.65 us
  local copies, waits for them, and re-layouts: 14.3 us -> 2.82 us
  matrix products: 10.2 us -> 0 us
    psum x2 -> x0, blocking collectives: 200 us -> none  [the longest x1 100 us: on_device(): lax.psum(jnp.sum(probs * gap, axis=1, keepdims=True), ('dp', 'vocab'))]
    all_gather x2 -> x0, waiting for transfers between devices: 115 us -> none  [the longest x1 66.8 us: on_device(): hidden_full = lax.all_gather(student_part, 'dp', axis=0, tiled=True)]
    pmax x1 -> x0, blocking collectives: 102 us -> none  [on_device(): lax.pmax((jnp.max(student_logits, axis=1, keepdims=True), jnp.max(teacher...]
    unnamed x12 -> x0, waiting for transfers between devices: 88.8 us -> none
    pallas_call x0 -> x1, Pallas kernels: none -> 87.6 us  [on_device(): pl.pallas_call(functools.partial(kernel, Z, Y, X), out_shape=(jax.ShapeDt...]
    unnamed x1 -> x0, blocking collectives: 59 us -> none
    all_gather x2 -> x0, blocking collectives: 50.1 us -> none  [the longest x1 28.4 us: on_device(): lax.all_gather(teacher_hidden, 'vocab', axis=1, tiled=True)]
    unnamed x9 -> x0, starting transfers between devices: 27.1 us -> none
  transfers between devices with their start and end apart: 11 -> 0, of which waited for: 3 -> 0; matrix products, arithmetic and copies ran while one was open for 2% -> 0% of each run, Pallas kernels for 0% -> 0%
where the time goes in v1:
time: 95.1 us; the launch traced here: 94.7 us
  Pallas kernels  87.6 us (92%)
  other arithmetic  3.57 us (4%)
  local copies, waits for them, and re-layouts  2.82 us (3%)
    pallas_call x1, Pallas kernels, on_device(): pl.pallas_call(functools.partial(kernel, Z, Y, X), out_shape=(jax.ShapeDt...  87.6 us
    unnamed x1, local copies, waits for them, and re-layouts  2.82 us

profile of v1, /device:TPU:2, one launch (start us, length us, event | category | flops | bytes accessed | tf_op | source)
XLA Modules:
  0.0 94.7 jit_solution(5782604333905992831)
XLA Ops:
  0.6 0.8 pad_select_fusion
  1.5 1.3 %fusion.1.own_ref = bf16[8,640]{1,0:T(8,128)(2,1)} fusion(bf16[6,256]{1,0:T(8,128)(2,1)} %param.5, bf16[8,384]{1,0:T(8,128)(2,1)S(1)} %pad_select_fusion), kind=kLoop, calls=%fused_computation.2 | loop fusion | flops 30720 | bytes 19456 | tf_op jit(solution)/shard_map/concatenate | solution.py:389
  2.8 87.6 %shard_map.59 = (bf16[8,384]{1,0:T(8,128)(2,1)}, bf16[176,5120]{1,0:T(8,128)(2,1)}) custom-call(bf16[8,640]{1,0:T(8,128)(2,1)} %fusion.1.own_ref, bf16[176,5120]{1,0:T(8,128)(2,1)} %sw_hbm.1, bf16[176,4096]{1,0:T(8,128)(2,1)} %tw_hbm.1), custom_call_target="tpu_custom_call" | custom-call | tf_op jit(solution)/shard_map/pallas_call | solution.py:430
  90.4 1.4 %slice_select_fusion = bf16[6,320]{1,0:T(8,128)(2,1)} fusion(bf16[8,384]{1,0:T(8,128)(2,1)} %get-tuple-element.4, pred[]{:T(512)S(6)} %eq.5), kind=kLoop, calls=%fused_computation.3 | loop fusion | flops 1920 | bytes 11521 | tf_op jit(solution)/shard_map/jit(_where)/select_n | solution.py:447
  91.9 2.8 %copy.7 = bf16[176,5120]{1,0:T(8,128)(2,1)} copy(bf16[176,5120]{1,0:T(8,128)(2,1)} %get-tuple-element.9) | data formatting | bytes 3604480
